TPU v7x, 128 devices: a whole 4x4x4 slice. The times are simulated.
128 devices in a mesh: exp: 4 (over x), tp: 32 (over z, y, core).
Axes of the slice: x: 4, y: 4, z: 4, core: 2. Of those that a mesh axis runs over, the one named last changes fastest.
Arguments:
- inputs: bfloat16 [1024, 4096], P(('exp', 'tp')), may hold values from -6 to 6
- conv_weight: float32 [4, 4096], replicated, may hold values from -3 to 3
- expert_ids: int32 [1024, 2], P(('exp', 'tp')), may hold values from 0 to 7, all different within a row; in each aligned block of 8 rows (0 to 7, 8 to 15, ...) at most 3 rows name the same one
- gate_values: float32 [1024, 2], P(('exp', 'tp')), may hold values from 0.25 to 1
- cotangent: bfloat16 [1024, 4096], P(('exp', 'tp')), may hold values from -6 to 6
- gate_weight: bfloat16 [8, 4096, 14336], P('exp', None, 'tp'), may hold values from -0.09375 to 0.09375
- up_weight: bfloat16 [8, 4096, 14336], P('exp', None, 'tp'), may hold values from -0.09375 to 0.09375
- down_weight: bfloat16 [8, 14336, 4096], P('exp', 'tp'), may hold values from -0.046875 to 0.046875
Outputs:
- result: bfloat16 [1024, 4096], P(('exp', 'tp'))
- grad_inputs: bfloat16 [1024, 4096], P(('exp', 'tp'))
Inputs may be any that keep to these rules, and one draw needn't show every extreme that they name: `expert_ids`: the experts of one token differ. Among the 8 tokens of one device no expert is named more than 3 times, a bound that some block reaches; every expert is named somewhere.
All inputs are finite; a program needn't handle non-finite values.
Results may differ from a plain program's by a relative error of at most 0.014.
Values may be sent and summed in bfloat16 or wider, within the bound.
A program may use at most 128 MiB of HBM per device.

v0:
```python
import jax
import jax.numpy as jnp
from jax import lax
from jax.sharding import PartitionSpec as P


def shifted(array, axis, by):
    size = lax.axis_size(axis)
    pairs = [(i, i + by) for i in range(size) if 0 <= i + by < size]
    return lax.ppermute(array, axis, pairs)


def expert_rows(rows_in, rows_grad, gate_weight, up_weight, down_weight):
    gate_pre = jnp.einsum(
        "mjsd,jdf->mjsf", rows_in, gate_weight, preferred_element_type=jnp.float32
    )
    up_pre = jnp.einsum("mjsd,jdf->mjsf", rows_in, up_weight, preferred_element_type=jnp.float32)
    sigmoid_gate = jax.nn.sigmoid(gate_pre)
    activated = gate_pre * sigmoid_gate
    hidden = (activated * up_pre).astype(jnp.bfloat16)
    forward_part = jnp.einsum(
        "mjsf,jfd->mjsd", hidden, down_weight, preferred_element_type=jnp.float32
    )
    back_hidden = jnp.einsum(
        "mjsd,jfd->mjsf", rows_grad, down_weight, preferred_element_type=jnp.float32
    )
    grad_gate = (
        back_hidden * up_pre * sigmoid_gate * (1.0 + gate_pre * (1.0 - sigmoid_gate))
    ).astype(jnp.bfloat16)
    grad_up = (back_hidden * activated).astype(jnp.bfloat16)
    backward_part = jnp.einsum(
        "mjsf,jdf->mjsd", grad_gate, gate_weight, preferred_element_type=jnp.float32
    ) + jnp.einsum("mjsf,jdf->mjsd", grad_up, up_weight, preferred_element_type=jnp.float32)
    return (forward_part, backward_part)


def per_device(
    inputs, conv_weight, expert_ids, gate_values, cotangent, gate_weight, up_weight, down_weight
):
    tok_rows = inputs.shape[0]
    model_width = inputs.shape[1]
    kernel = conv_weight.shape[0]
    top_count = expert_ids.shape[1]
    groups = lax.axis_size("exp")
    per_group = gate_weight.shape[0]
    experts = groups * per_group
    slot_count = tok_rows * top_count * 3 // (2 * experts)
    source = inputs.astype(jnp.float32)
    rim_rows = shifted(inputs[tok_rows - (kernel - 1) :], ("exp", "tp"), 1)
    extended = jnp.concatenate([rim_rows.astype(jnp.float32), source], 0)
    conv_sum = source
    for shift_step in range(kernel):
        conv_sum = (
            conv_sum
            + conv_weight[shift_step]
            * extended[kernel - 1 - shift_step : kernel - 1 - shift_step + tok_rows]
        )
    mixed = conv_sum.astype(jnp.bfloat16)
    flat_ids = expert_ids.reshape(-1)
    onehot_ids = (flat_ids[:, None] == jnp.arange(experts, dtype=jnp.int32)[None, :]).astype(
        jnp.int32
    )
    earlier = jnp.cumsum(onehot_ids, 0) - onehot_ids
    slot_index = jnp.sum(earlier * onehot_ids, 1)
    target = flat_ids * slot_count + slot_index
    places = (
        jnp.arange(experts * slot_count, dtype=jnp.int32)[:, None] == target[None, :]
    ).reshape(experts * slot_count, tok_rows, top_count)
    dispatch_map = jnp.any(places, 2).astype(jnp.bfloat16)
    packed_in = (
        jnp.dot(dispatch_map, mixed, preferred_element_type=jnp.float32)
        .astype(jnp.bfloat16)
        .reshape(groups, per_group, slot_count, model_width)
    )
    packed_grad = (
        jnp.dot(dispatch_map, cotangent, preferred_element_type=jnp.float32)
        .astype(jnp.bfloat16)
        .reshape(groups, per_group, slot_count, model_width)
    )
    recv_in, recv_grad = (
        lax.all_to_all(packed_in, "exp", split_axis=0, concat_axis=0, tiled=True),
        lax.all_to_all(packed_grad, "exp", split_axis=0, concat_axis=0, tiled=True),
    )
    stacked = jnp.stack([recv_in, recv_grad], 0)[None]
    piece = lax.all_gather(stacked, "tp", axis=0, tiled=True)
    piece_rows = piece.shape[0]
    rows_in = piece[:, 0].reshape(piece_rows * groups, per_group, slot_count, model_width)
    rows_grad = piece[:, 1].reshape(piece_rows * groups, per_group, slot_count, model_width)
    forward_part, backward_part = expert_rows(
        rows_in, rows_grad, gate_weight, up_weight, down_weight
    )
    shape_back = (piece_rows, groups, per_group, slot_count, model_width)
    partials = jnp.stack(
        [
            forward_part.astype(jnp.bfloat16).reshape(shape_back),
            backward_part.astype(jnp.bfloat16).reshape(shape_back),
        ],
        1,
    )
    summed = lax.psum(partials, "tp").astype(jnp.float32)
    own_sums = lax.dynamic_index_in_dim(summed, lax.axis_index("tp"), 0, keepdims=False)
    returned = lax.all_to_all(
        own_sums.astype(jnp.bfloat16), "exp", split_axis=1, concat_axis=1, tiled=True
    ).astype(own_sums.dtype)
    expert_out = returned[0].reshape(experts * slot_count, model_width)
    expert_back = returned[1].reshape(experts * slot_count, model_width)
    picked_out = jnp.take(expert_out, target, axis=0).reshape(tok_rows, top_count, model_width)
    picked_back = jnp.take(expert_back, target, axis=0).reshape(tok_rows, top_count, model_width)
    moe_out = jnp.sum(picked_out * gate_values[:, :, None], 1)
    moe_back = jnp.sum(picked_back * gate_values[:, :, None], 1)
    result = (mixed.astype(jnp.float32) + moe_out).astype(jnp.bfloat16)
    grad_mixed = cotangent.astype(jnp.float32) + moe_back
    next_rows = shifted(grad_mixed[: kernel - 1].astype(jnp.bfloat16), ("exp", "tp"), -1).astype(
        jnp.float32
    )
    extended_grad = jnp.concatenate([grad_mixed, next_rows], 0)
    grad_sum = grad_mixed
    for shift_step in range(kernel):
        grad_sum = (
            grad_sum + conv_weight[shift_step] * extended_grad[shift_step : shift_step + tok_rows]
        )
    return (result, grad_sum.astype(jnp.bfloat16))


def solution(mesh):
    in_specs = (
        P(("exp", "tp"), None),
        P(),
        P(("exp", "tp"), None),
        P(("exp", "tp"), None),
        P(("exp", "tp"), None),
        P("exp", None, "tp"),
        P("exp", None, "tp"),
        P("exp", "tp", None),
    )
    out_specs = (P(("exp", "tp"), None), P(("exp", "tp"), None))
    return jax.shard_map(
        per_device, mesh=mesh, in_specs=in_specs, out_specs=out_specs, check_vma=False
    )
```

profile of v0, /device:TPU:121, one launch (start us, length us, event | category | flops | bytes accessed | tf_op | source)
XLA Modules:
  0.0 404.0 jit_solution(1930475148583040575)
XLA Ops:
  7.2 0.9 slice.55
  8.0 2.0 collective-permute-start
  10.0 0.8 copy.36
  10.8 0.1 eq.30
  10.8 0.1 fusion.52
  11.0 0.2 select_reduce_fusion
  11.1 0.1 reduce_sum.30
  11.2 0.1 copy.38
  11.3 0.1 fusion.53
  11.4 1.1 convolution_convert_fusion
  12.5 0.1 reshape.43
  12.6 0.9 copy.40
  13.6 4.0 all-to-all-start.1
  17.5 1.1 fusion.59
  18.6 0.9 convert_element_type.68
  19.4 0.0 collective-permute-done
  19.5 0.1 fusion.37
  19.6 0.2 convolution_convert_fusion.1
  19.8 0.1 reshape.42
  20.0 0.2 copy.39
  20.2 2.5 all-to-all-done.1
  22.7 7.5 %all_to_all.15 = bf16[4,2,3,4096]{3,1,2,0:T(2,128)(2,1)S(1)} all-to-all(bf16[4,2,3,4096]{3,1,2,0:T(2,128)(2,1)S(1)} %copy.39), channel_id=1, replica_groups=mesh['exp'=4,'tp'=32] {'exp'}, dimensions={0} | all-to-all | bytes 393216 | tf_op jit(solution)/shard_map/all_to_all | solution.py:81
  30.2 0.6 pad_maximum_fusion.1
  30.8 1.1 copy.41
  31.9 0.0 all-gather.3.cloned.1.call-update
  31.9 0.2 all-reduce.2.cloned.1.call-start
  32.1 64.0 %all-gather.3.cloned.1.call-done = bf16[64,4,2,3,4096]{4,1,3,2,0:T(4,128)(2,1)} async-done(((bf16[2,4,2,3,4096]{4,1,3,2,0:T(4,128)(2,1)}), bf16[64,4,2,3,4096]{4,1,3,2,0:T(4,128)(2,1)}) %all-gather.3.cloned.1.call-update) | async-done | bytes 12582928 | tf_op jit(solution)/shard_map/all_gather | solution.py:85
  96.1 11.2 %fusion.57 = (bf16[32,1,4,2,3,4096]{5,2,4,3,1,0:T(4,128)(2,1)}, bf16[32,1,4,2,3,4096]{5,2,4,3,1,0:T(4,128)(2,1)S(1)}) fusion(bf16[32,2,4,2,3,4096]{5,2,4,3,1,0:T(4,128)(2,1)} %bitcast.69), kind=kLoop, calls=%fused_computation.81 | loop fusion | bytes 25165824 | tf_op jit(solution)/shard_map/slice | solution.py:88
  107.3 5.7 %copy.54 = bf16[32,1,4,2,3,4096]{5,2,0,4,3,1:T(4,128)(2,1)} copy(bf16[32,1,4,2,3,4096]{5,2,4,3,1,0:T(4,128)(2,1)S(1)} %get-tuple-element.8) | data formatting | bytes 12582912
  113.0 9.7 %reshape_squeeze.12 = bf16[128,2,3,4096]{3,0,2,1:T(8,128)(2,1)} reshape(bf16[32,1,4,2,3,4096]{5,2,0,4,3,1:T(4,128)(2,1)} %copy.54) | data formatting | bytes 12582912 | tf_op jit(solution)/shard_map/reshape;squeeze | solution.py:87
  122.7 9.4 %fusion.23 = f32[128,2,3,448]{0,3,2,1:T(8,128)} fusion(bf16[128,2,3,4096]{3,0,2,1:T(8,128)(2,1)} %reshape_squeeze.12, bf16[2,4096,448]{1,2,0:T(8,128)(2,1)} %param.15), kind=kOutput, calls=%fused_computation.21 | convolution fusion | flops 2818572288 | bytes 15007744 | tf_op jit(solution)/shard_map/mjsd,jdf->mjsf/dot_general | solution.py:14
  132.1 7.2 %fusion.26 = f32[128,2,3,448]{0,3,2,1:T(8,128)} fusion(bf16[128,2,3,4096]{3,0,2,1:T(8,128)(2,1)S(1)} %copy-done.1, bf16[2,4096,448]{1,2,0:T(8,128)(2,1)} %param.16), kind=kOutput, calls=%fused_computation.22 | convolution fusion | flops 2818572288 | bytes 15007744 | tf_op jit(solution)/shard_map/mjsd,jdf->mjsf/dot_general | solution.py:17
  139.4 5.7 %copy.55 = bf16[32,1,4,2,3,4096]{5,2,0,4,3,1:T(4,128)(2,1)} copy(bf16[32,1,4,2,3,4096]{5,2,4,3,1,0:T(4,128)(2,1)S(1)} %bitcast.66) | data formatting | bytes 12582912
  145.1 9.9 %reshape_squeeze.13 = bf16[128,2,3,4096]{3,0,2,1:T(8,128)(2,1)} reshape(bf16[32,1,4,2,3,4096]{5,2,0,4,3,1:T(4,128)(2,1)} %copy.55) | data formatting | bytes 12582912 | tf_op jit(solution)/shard_map/reshape;squeeze | solution.py:88
  155.0 8.7 %fusion.20 = f32[128,2,3,448]{0,3,2,1:T(8,128)S(1)} fusion(bf16[128,2,3,4096]{3,0,2,1:T(8,128)(2,1)} %reshape_squeeze.13, bf16[2,448,4096]{2,1,0:T(8,128)(2,1)} %param.17), kind=kOutput, calls=%fused_computation.20 | convolution fusion | flops 2818572288 | bytes 15007744 | tf_op jit(solution)/shard_map/mjsd,jfd->mjsf/dot_general | solution.py:24
  163.6 9.8 %fusion.17 = bf16[128,2,3,4096]{3,0,2,1:T(8,128)(2,1)} fusion(bf16[2,448,4096]{2,1,0:T(8,128)(2,1)} %param.17, f32[128,2,3,448]{0,3,2,1:T(8,128)S(1)} %copy-done.4, f32[128,2,3,448]{0,3,2,1:T(8,128)S(1)} %copy-done.2), kind=kOutput, calls=%fused_computation.17 | convolution fusion | flops 2823782400 | bytes 16384000 | tf_op jit(solution)/shard_map/mjsf,jfd->mjsd/dot_general | solution.py:21
  173.4 6.6 %fusion.3 = f32[2,128,3,4096]{3,1,2,0:T(8,128)} fusion(bf16[2,4096,448]{1,2,0:T(8,128)(2,1)S(1)} %bitcast.71, f32[128,2,3,448]{0,3,2,1:T(8,128)S(1)} %copy-done.2, f32[128,2,3,448]{0,3,2,1:T(8,128)S(1)} %fusion.20, f32[128,2,3,448]{0,3,2,1:T(8,128)S(1)} %copy-done.4), kind=kOutput, calls=%fused_computation.7 | convolution fusion | flops 2822012928 | bytes 24051712 | tf_op jit(solution)/shard_map/mjsf,jdf->mjsd/dot_general | solution.py:31
  180.1 11.1 %fusion.14 = bf16[128,2,3,4096]{3,0,2,1:T(8,128)(2,1)S(1)} fusion(f32[2,128,3,4096]{3,1,2,0:T(8,128)} %fusion.3, bf16[2,4096,448]{1,2,0:T(8,128)(2,1)} %param.16, f32[128,2,3,448]{0,3,2,1:T(8,128)} %copy-done.3, f32[128,2,3,448]{0,3,2,1:T(8,128)} %fusion.23), kind=kOutput, calls=%fused_computation.16 | convolution fusion | flops 2826928128 | bytes 28966912 | tf_op jit(solution)/shard_map/mjsf,jdf->mjsd/dot_general | solution.py:33
  191.2 12.8 %copy.53 = bf16[128,2,3,4096]{3,1,2,0:T(2,128)(2,1)S(1)} copy(bf16[128,2,3,4096]{3,0,2,1:T(8,128)(2,1)S(1)} %fusion.14) | data formatting | bytes 12582912 | tf_op jit(solution)/shard_map/stack;reshape | solution.py:93
  204.1 12.8 %copy.52 = bf16[128,2,3,4096]{3,1,2,0:T(2,128)(2,1)S(1)} copy(bf16[128,2,3,4096]{3,0,2,1:T(8,128)(2,1)S(1)} %copy-done) | data formatting | bytes 12582912 | tf_op jit(solution)/shard_map/stack;reshape | solution.py:93
  216.9 18.0 %pad_maximum_fusion = bf16[32,2,4,2,3,4096]{5,3,4,1,2,0:T(2,128)(2,1)} fusion(bf16[32,1,4,2,3,4096]{5,3,4,1,2,0:T(2,128)(2,1)S(1)} %bitcast.67, bf16[32,1,4,2,3,4096]{5,3,4,1,2,0:T(2,128)(2,1)S(1)} %bitcast.68), kind=kLoop, calls=%fused_computation.2 | loop fusion | flops 6291456 | bytes 25165824 | tf_op jit(solution)/shard_map/stack | solution.py:93
  234.9 0.0 all-reduce.2.cloned.1.call-update
  235.0 0.6 copy-done.6
  235.6 0.1 copy.47
  235.7 133.0 %all-reduce.2.cloned.1.call-done = bf16[32,2,4,2,3,4096]{5,3,4,1,2,0:T(2,128)(2,1)} async-done(((bf16[32,2,4,2,3,4096]{5,3,4,1,2,0:T(2,128)(2,1)}), bf16[32,2,4,2,3,4096]{5,3,4,1,2,0:T(2,128)(2,1)}) %all-reduce.2.cloned.1.call-update) | async-done | bytes 12582928 | tf_op jit(solution)/shard_map/psum | solution.py:100
  368.7 2.2 fusion.31
  370.8 4.0 all-to-all-start.2
  374.8 0.0 copy-start.5
  374.8 8.4 %all-to-all-done.2 = bf16[2,4,2,3,4096]{4,2,3,0,1:T(2,128)(2,1)S(1)} async-done(((bf16[2,4,2,3,4096]{4,2,3,0,1:T(2,128)(2,1)}), bf16[2,4,2,3,4096]{4,2,3,0,1:T(2,128)(2,1)S(1)}, u32[]{:S(2)}, u32[]{:S(2)}) %all-to-all-start.2) | async-done | bytes 393248 | tf_op jit(solution)/shard_map/all_to_all | solution.py:102
  383.2 0.3 fusion.58
  383.5 0.3 copy.48
  383.8 0.2 reshape_squeeze.15
  384.0 0.3 copy.46
  384.3 0.2 reshape_squeeze.14
  384.5 0.6 gather_fusion.1
  385.1 0.6 gather_fusion
  385.8 0.1 broadcast_select_fusion.1
  385.9 0.2 reshape.44
  386.1 0.2 reshape.45
  386.2 0.7 multiply_reduce_fusion
  387.0 2.5 collective-permute-start.1
  389.5 0.6 add_convert_fusion.1
  390.2 6.2 %collective-permute-done.1 = bf16[3,4096]{1,0:T(4,128)(2,1)S(1)} collective-permute-done((bf16[3,4096]{1,0:T(4,128)(2,1)S(1)}, bf16[3,4096]{1,0:T(4,128)(2,1)S(1)}, u32[]{:S(2)}, u32[]{:S(2)}) %collective-permute-start.1) | collective-permute-done | bytes 24608 | tf_op jit(solution)/shard_map/ppermute | solution.py:10
  396.4 0.7 fusion.41
  (31 shorter events, 0.1 us)
Async XLA Ops:
  8.0 11.4 %collective-permute-start = (bf16[3,4096]{1,0:T(4,128)(2,1)S(1)}, bf16[3,4096]{1,0:T(4,128)(2,1)S(1)}, u32[]{:S(2)}, u32[]{:S(2)}) collective-permute-start(bf16[3,4096]{1,0:T(4,128)(2,1)S(1)} %slice.55), channel_id=1, source_target_pairs={{0,1},{1,2},{2,3},{3,4},{4,5},{5,6},{6,7},{7,8},{8,9},{9,10},{10,1... | collective-permute-start | bytes 73736 | tf_op jit(solution)/shard_map/ppermute | solution.py:10
  13.6 9.1 %all-to-all-start.1 = ((bf16[4,2,3,4096]{3,1,2,0:T(2,128)(2,1)}), bf16[4,2,3,4096]{3,1,2,0:T(2,128)(2,1)S(1)}, u32[]{:S(2)}, u32[]{:S(2)}) async-start(bf16[4,2,3,4096]{3,1,2,0:T(2,128)(2,1)} %copy.40), calls=%async_computation.1 | async-start | bytes 393216 | tf_op jit(solution)/shard_map/all_to_all | solution.py:82
  17.5 78.6 %all-gather.3.cloned.1.call-start = ((), (), s32[]{:S(2)}) async-start(), calls=%async_computation.4 | async-start | bytes 12976128 | tf_op jit(solution)/shard_map/all_gather | solution.py:85
  31.9 336.8 %all-reduce.2.cloned.1.call-start = ((), (), s32[]{:S(2)}) async-start(), calls=%async_computation.3 | async-start | bytes 25165824 | tf_op jit(solution)/shard_map/psum | solution.py:100
  122.7 9.4 %copy-start.1 = (bf16[128,2,3,4096]{3,0,2,1:T(8,128)(2,1)S(1)}, bf16[128,2,3,4096]{3,0,2,1:T(8,128)(2,1)}, u32[]{:S(2)}) copy-start(bf16[128,2,3,4096]{3,0,2,1:T(8,128)(2,1)} %reshape_squeeze.12) | copy-start | bytes 18874372
  122.7 16.7 %slice-start = ((s8[6291456]{0:T(1024)(128)(4,1)}), s8[4194304]{0:T(1024)(128)(4,1)S(1)}, s32[]{:S(2)}) async-start(s8[6291456]{0:T(1024)(128)(4,1)} %bitcast.65), calls=%async_computation.5 | async-start | bytes 8388608
  132.1 7.2 %slice-start.1 = ((s8[6291456]{0:T(1024)(128)(4,1)}), s8[2097152]{0:T(1024)(128)(4,1)S(1)}, s32[]{:S(2)}) async-start(s8[6291456]{0:T(1024)(128)(4,1)} %bitcast.65), calls=%async_computation.6 | async-start | bytes 4194304
  145.1 28.3 %slice-start.2 = ((s8[7340032]{0:T(1024)(128)(4,1)}), s8[3145728]{0:T(1024)(128)(4,1)S(1)}, s32[]{:S(2)}) async-start(s8[7340032]{0:T(1024)(128)(4,1)} %bitcast.70), calls=%async_computation.7 | async-start | bytes 6291456
  155.0 8.7 %copy-start.2 = (f32[128,2,3,448]{0,3,2,1:T(8,128)S(1)}, f32[128,2,3,448]{0,3,2,1:T(8,128)}, u32[]{:S(2)}) copy-start(f32[128,2,3,448]{0,3,2,1:T(8,128)} %fusion.23) | copy-start | bytes 4128772
  155.0 8.7 %copy-start.4 = (f32[128,2,3,448]{0,3,2,1:T(8,128)S(1)}, f32[128,2,3,448]{0,3,2,1:T(8,128)}, u32[]{:S(2)}) copy-start(f32[128,2,3,448]{0,3,2,1:T(8,128)} %fusion.26) | copy-start | bytes 4128772
  155.0 18.5 %slice-start.3 = ((s8[7340032]{0:T(1024)(128)(4,1)}), s8[4194304]{0:T(1024)(128)(4,1)S(1)}, s32[]{:S(2)}) async-start(s8[7340032]{0:T(1024)(128)(4,1)} %bitcast.70), calls=%async_computation.8 | async-start | bytes 8388608
  163.6 9.8 %copy-start.3 = (f32[128,2,3,448]{0,3,2,1:T(8,128)}, f32[128,2,3,448]{0,3,2,1:T(8,128)S(1)}, u32[]{:S(2)}) copy-start(f32[128,2,3,448]{0,3,2,1:T(8,128)S(1)} %fusion.20) | copy-start | bytes 4128772
  191.2 12.9 %copy-start = (bf16[128,2,3,4096]{3,0,2,1:T(8,128)(2,1)S(1)}, bf16[128,2,3,4096]{3,0,2,1:T(8,128)(2,1)}, u32[]{:S(2)}) copy-start(bf16[128,2,3,4096]{3,0,2,1:T(8,128)(2,1)} %fusion.17) | copy-start | bytes 18874372
  234.9 0.7 copy-start.6
  370.8 12.4 %all-to-all-start.2 = ((bf16[2,4,2,3,4096]{4,2,3,0,1:T(2,128)(2,1)}), bf16[2,4,2,3,4096]{4,2,3,0,1:T(2,128)(2,1)S(1)}, u32[]{:S(2)}, u32[]{:S(2)}) async-start(bf16[2,4,2,3,4096]{4,2,3,0,1:T(2,128)(2,1)} %fusion.31), calls=%async_computation.2 | async-start | bytes 786432 | tf_op jit(solution)/shard_map/all_to_all | solution.py:102
  374.8 12.1 %copy-start.5 = (bf16[8,4096]{1,0:T(8,128)(2,1)S(1)}, bf16[8,4096]{1,0:T(8,128)(2,1)}, u32[]{:S(2)}) copy-start(bf16[8,4096]{1,0:T(8,128)(2,1)} %param.14) | copy-start | bytes 196612
  387.0 9.5 %collective-permute-start.1 = (bf16[3,4096]{1,0:T(4,128)(2,1)S(1)}, bf16[3,4096]{1,0:T(4,128)(2,1)S(1)}, u32[]{:S(2)}, u32[]{:S(2)}) collective-permute-start(bf16[3,4096]{1,0:T(4,128)(2,1)S(1)} %slice.127), channel_id=1, source_target_pairs={{1,0},{2,1},{3,2},{4,3},{5,4},{6,5},{7,6},{8,7},{9,8},{10,9},{11,1... | collective-permute-start | bytes 73736 | tf_op jit(solution)/shard_map/ppermute | solution.py:10
Sparse Core Ops, SparseCore 0:
  32.0 64.0 all-gather.2
  235.1 133.5 all-reduce.1
where the time goes:
time: 405 us; the launch traced here: 404 us
  waiting for transfers between devices  214 us (53%)
  local copies, waits for them, and re-layouts  76.9 us (19%)
  matrix products  54.2 us (13%)
  other arithmetic  24.4 us (6%)
  between operations  14.3 us (4%)
  starting transfers between devices  12.7 us (3%)
  blocking collectives  7.53 us (2%)
    psum x1, waiting for transfers between devices, per_device(): summed = lax.psum(partials, 'tp').astype(jnp.float32)  133 us
    all_gather x1, waiting for transfers between devices, per_device(): piece = lax.all_gather(stacked, 'tp', axis=0, tiled=True)  64 us
    another operation x2, local copies, waits for them, and re-layouts, per_device(): jnp.stack([forward_part.astype(jnp.bfloat16).reshape(shape_back), backwar...  25.7 us
    another operation x1, other arithmetic, per_device(): jnp.stack([forward_part.astype(jnp.bfloat16).reshape(shape_back), backwar...  18 us
    unnamed x26, local copies, waits for them, and re-layouts  13 us
    slice x1, local copies, waits for them, and re-layouts, per_device(): piece[:, 1].reshape(piece_rows * groups, per_group, slot_count, model_width)  11.2 us
    dot_general x1, matrix products, expert_rows(): jnp.einsum('mjsf,jdf->mjsd', grad_up, up_weight, preferred_element_type=j...  11.1 us
    another operation x1, local copies, waits for them, and re-layouts, per_device(): piece[:, 1].reshape(piece_rows * groups, per_group, slot_count, model_width)  9.86 us
  transfers between devices with their start and end apart: 6, of which 5 were waited for; matrix products, arithmetic and copies ran while one was open for 2% of the time, Pallas kernels for 0%

commit v1 on v0

--- a/solution.py
+++ b/solution.py
@@ -82,7 +82,9 @@
         lax.all_to_all(packed_grad, "exp", split_axis=0, concat_axis=0, tiled=True),
     )
     stacked = jnp.stack([recv_in, recv_grad], 0)[None]
-    piece = lax.all_gather(stacked, "tp", axis=0, tiled=True)
+    piece = jnp.concatenate(
+        lax.all_to_all(jnp.stack([stacked] * lax.axis_size("tp")), "tp", 0, 0), axis=0
+    )
     piece_rows = piece.shape[0]
     rows_in = piece[:, 0].reshape(piece_rows * groups, per_group, slot_count, model_width)
     rows_grad = piece[:, 1].reshape(piece_rows * groups, per_group, slot_count, model_width)

time: 405 us -> 490 us (1.21)
  blocking collectives: 7.53 us -> 158 us
  waiting for transfers between devices: 214 us -> 148 us
    all_to_all x0 -> x1, blocking collectives: none -> 151 us  [per_device(): lax.all_to_all(jnp.stack([stacked] * lax.axis_size('tp')), 'tp', 0, 0)]
    all_gather x1 -> x0, waiting for transfers between devices: 64 us -> none  [per_device(): piece = lax.all_gather(stacked, 'tp', axis=0, tiled=True)]
    unnamed x26 -> x24, local copies, waits for them, and re-layouts: 13 us -> 1.53 us
    another operation x0 -> x1, local copies, waits for them, and re-layouts: none -> 5.88 us  [per_device(): jnp.stack([stacked] * lax.axis_size('tp'))]
    slice x0 -> x1, local copies, waits for them, and re-layouts: none -> 5.66 us  [per_device(): piece[:, 0].reshape(piece_rows * groups, per_group, slot_count, model_width)]
    slice x1 -> x2, local copies, waits for them, and re-layouts: 11.2 us -> 12.1 us  [per_device(): piece[:, 1].reshape(piece_rows * groups, per_group, slot_count, model_width)]
  transfers between devices with their start and end apart: 6 -> 5, of which waited for: 5 -> 4; matrix products, arithmetic and copies ran while one was open for 2% -> 1% of each run, Pallas kernels for 0% -> 0%
where the time goes in v1:
time: 490 us; the launch traced here: 489 us
  blocking collectives  158 us (32%)
  waiting for transfers between devices  148 us (30%)
  local copies, waits for them, and re-layouts  77.1 us (16%)
  matrix products  54.4 us (11%)
  other arithmetic  24.3 us (5%)
  between operations  14.3 us (3%)
  starting transfers between devices  12.5 us (3%)
    all_to_all x1, blocking collectives, per_device(): lax.all_to_all(jnp.stack([stacked] * lax.axis_size('tp')), 'tp', 0, 0)  151 us
    psum x1, waiting for transfers between devices, per_device(): summed = lax.psum(partials, 'tp').astype(jnp.float32)  131 us
    another operation x2, local copies, waits for them, and re-layouts, per_device(): jnp.stack([forward_part.astype(jnp.bfloat16).reshape(shape_back), backwar...  25.7 us
    another operation x1, other arithmetic, per_device(): jnp.stack([forward_part.astype(jnp.bfloat16).reshape(shape_back), backwar...  18 us
    slice x2, local copies, waits for them, and re-layouts, per_device(): piece[:, 1].reshape(piece_rows * groups, per_group, slot_count, model_width)  12.1 us
    dot_general x1, matrix products, expert_rows(): jnp.einsum('mjsf,jdf->mjsd', grad_up, up_weight, preferred_element_type=j...  11.1 us
    another operation x1, local copies, waits for them, and re-layouts, per_device(): piece[:, 1].reshape(piece_rows * groups, per_group, slot_count, model_width)  9.85 us
  transfers between devices with their start and end apart: 5, of which 4 were waited for; matrix products, arithmetic and copies ran while one was open for 1% of the time, Pallas kernels for 0%

profile of v1, /device:TPU:121, one launch (start us, length us, event | category | flops | bytes accessed | tf_op | source)
XLA Modules:
  0.0 488.8 jit_solution(470950605922124631)
XLA Ops:
  7.2 0.9 slice.55
  8.0 2.0 collective-permute-start
  10.0 0.8 copy.34
  10.8 0.1 eq.30
  10.8 0.1 fusion.52
  11.0 0.2 select_reduce_fusion
  11.1 0.1 reduce_sum.30
  11.2 0.1 copy.36
  11.3 0.1 fusion.53
  11.4 1.1 convolution_convert_fusion
  12.5 0.1 reshape.48
  12.6 0.9 copy.38
  13.6 4.0 all-to-all-start.1
  17.5 1.1 fusion.59
  18.6 0.9 convert_element_type.68
  19.4 0.0 collective-permute-done
  19.5 0.1 fusion.37
  19.6 0.2 convolution_convert_fusion.1
  19.8 0.1 reshape.47
  20.0 0.2 copy.37
  20.2 2.5 all-to-all-done.1
  22.7 7.5 %all_to_all.20 = bf16[4,2,3,4096]{3,1,2,0:T(2,128)(2,1)S(1)} all-to-all(bf16[4,2,3,4096]{3,1,2,0:T(2,128)(2,1)S(1)} %copy.37), channel_id=1, replica_groups=mesh['exp'=4,'tp'=32] {'exp'}, dimensions={0} | all-to-all | bytes 393216 | tf_op jit(solution)/shard_map/all_to_all | solution.py:81
  30.2 0.6 pad_maximum_fusion.1
  30.8 0.3 copy.39
  31.1 5.9 %stack.18 = bf16[32,1,2,4,2,3,4096]{6,3,5,4,2,1,0:T(4,128)(2,1)S(1)} broadcast(bf16[2,4,2,3,4096]{4,1,3,2,0:T(4,128)(2,1)S(1)} %copy.39), dimensions={2,3,4,5,6} | broadcast | bytes 12976128 | tf_op jit(solution)/shard_map/stack | solution.py:86
  37.0 150.6 %all_to_all.21 = bf16[32,1,2,4,2,3,4096]{6,3,5,4,2,1,0:T(4,128)(2,1)S(1)} all-to-all(bf16[32,1,2,4,2,3,4096]{6,3,5,4,2,1,0:T(4,128)(2,1)S(1)} %stack.18), channel_id=1, replica_groups=mesh['exp'=4,'tp'=32] {'tp'}, dimensions={0} | all-to-all | bytes 25165824 | tf_op jit(solution)/shard_map/all_to_all | solution.py:86
  187.6 6.4 %fusion.57 = (bf16[32,1,4,2,3,4096]{5,2,4,3,1,0:T(4,128)(2,1)}, bf16[32,1,4,2,3,4096]{5,2,4,3,1,0:T(4,128)(2,1)S(1)}) fusion(bf16[32,2,4,2,3,4096]{5,2,4,3,1,0:T(4,128)(2,1)S(1)} %bitcast.65), kind=kLoop, calls=%fused_computation.81 | loop fusion | bytes 25165824 | tf_op jit(solution)/shard_map/slice | solution.py:90
  194.0 5.7 %copy.40 = bf16[32,1,4,2,3,4096]{5,2,0,4,3,1:T(4,128)(2,1)} copy(bf16[32,1,4,2,3,4096]{5,2,4,3,1,0:T(4,128)(2,1)S(1)} %get-tuple-element.8) | data formatting | bytes 12582912 | tf_op jit(solution)/shard_map/slice | solution.py:89
  199.6 9.7 %reshape_squeeze.12 = bf16[128,2,3,4096]{3,0,2,1:T(8,128)(2,1)} reshape(bf16[32,1,4,2,3,4096]{5,2,0,4,3,1:T(4,128)(2,1)} %copy.40) | data formatting | bytes 12582912 | tf_op jit(solution)/shard_map/reshape;squeeze | solution.py:89
  209.4 9.7 %fusion.23 = f32[128,2,3,448]{0,3,2,1:T(8,128)} fusion(bf16[128,2,3,4096]{3,0,2,1:T(8,128)(2,1)} %reshape_squeeze.12, bf16[2,4096,448]{1,2,0:T(8,128)(2,1)} %param.15), kind=kOutput, calls=%fused_computation.21 | convolution fusion | flops 2818572288 | bytes 15007744 | tf_op jit(solution)/shard_map/mjsd,jdf->mjsf/dot_general | solution.py:14
  219.1 0.0 copy-done.1
  219.1 7.2 %fusion.26 = f32[128,2,3,448]{0,3,2,1:T(8,128)} fusion(bf16[128,2,3,4096]{3,0,2,1:T(8,128)(2,1)S(1)} %copy-done.1, bf16[2,4096,448]{1,2,0:T(8,128)(2,1)} %param.16), kind=kOutput, calls=%fused_computation.22 | convolution fusion | flops 2818572288 | bytes 15007744 | tf_op jit(solution)/shard_map/mjsd,jdf->mjsf/dot_general | solution.py:17
  226.3 5.7 %copy.41 = bf16[32,1,4,2,3,4096]{5,2,0,4,3,1:T(4,128)(2,1)} copy(bf16[32,1,4,2,3,4096]{5,2,4,3,1,0:T(4,128)(2,1)S(1)} %bitcast.67) | data formatting | bytes 12582912 | tf_op jit(solution)/shard_map/slice | solution.py:90
  232.0 9.8 %reshape_squeeze.13 = bf16[128,2,3,4096]{3,0,2,1:T(8,128)(2,1)} reshape(bf16[32,1,4,2,3,4096]{5,2,0,4,3,1:T(4,128)(2,1)} %copy.41) | data formatting | bytes 12582912 | tf_op jit(solution)/shard_map/reshape;squeeze | solution.py:90
  241.9 8.7 %fusion.20 = f32[128,2,3,448]{0,3,2,1:T(8,128)S(1)} fusion(bf16[128,2,3,4096]{3,0,2,1:T(8,128)(2,1)} %reshape_squeeze.13, bf16[2,448,4096]{2,1,0:T(8,128)(2,1)} %param.17), kind=kOutput, calls=%fused_computation.20 | convolution fusion | flops 2818572288 | bytes 15007744 | tf_op jit(solution)/shard_map/mjsd,jfd->mjsf/dot_general | solution.py:24
  250.6 9.8 %fusion.17 = bf16[128,2,3,4096]{3,0,2,1:T(8,128)(2,1)} fusion(bf16[2,448,4096]{2,1,0:T(8,128)(2,1)} %param.17, f32[128,2,3,448]{0,3,2,1:T(8,128)S(1)} %copy-done.4, f32[128,2,3,448]{0,3,2,1:T(8,128)S(1)} %copy-done.2), kind=kOutput, calls=%fused_computation.17 | convolution fusion | flops 2823782400 | bytes 16384000 | tf_op jit(solution)/shard_map/mjsf,jfd->mjsd/dot_general | solution.py:21
  260.3 6.6 %fusion.3 = f32[2,128,3,4096]{3,1,2,0:T(8,128)} fusion(bf16[2,4096,448]{1,2,0:T(8,128)(2,1)S(1)} %bitcast.71, f32[128,2,3,448]{0,3,2,1:T(8,128)S(1)} %copy-done.2, f32[128,2,3,448]{0,3,2,1:T(8,128)S(1)} %fusion.20, f32[128,2,3,448]{0,3,2,1:T(8,128)S(1)} %copy-done.4), kind=kOutput, calls=%fused_computation.7 | convolution fusion | flops 2822012928 | bytes 24051712 | tf_op jit(solution)/shard_map/mjsf,jdf->mjsd/dot_general | solution.py:31
  267.0 11.1 %fusion.14 = bf16[128,2,3,4096]{3,0,2,1:T(8,128)(2,1)S(1)} fusion(f32[2,128,3,4096]{3,1,2,0:T(8,128)} %fusion.3, bf16[2,4096,448]{1,2,0:T(8,128)(2,1)} %param.16, f32[128,2,3,448]{0,3,2,1:T(8,128)} %copy-done.3, f32[128,2,3,448]{0,3,2,1:T(8,128)} %fusion.23), kind=kOutput, calls=%fused_computation.16 | convolution fusion | flops 2826928128 | bytes 28966912 | tf_op jit(solution)/shard_map/mjsf,jdf->mjsd/dot_general | solution.py:33
  278.1 12.8 %copy.51 = bf16[128,2,3,4096]{3,1,2,0:T(2,128)(2,1)S(1)} copy(bf16[128,2,3,4096]{3,0,2,1:T(8,128)(2,1)S(1)} %fusion.14) | data formatting | bytes 12582912 | tf_op jit(solution)/shard_map/stack;reshape | solution.py:95
  291.0 12.8 %copy.50 = bf16[128,2,3,4096]{3,1,2,0:T(2,128)(2,1)S(1)} copy(bf16[128,2,3,4096]{3,0,2,1:T(8,128)(2,1)S(1)} %copy-done) | data formatting | bytes 12582912 | tf_op jit(solution)/shard_map/stack;reshape | solution.py:95
  303.8 18.0 %pad_maximum_fusion = bf16[32,2,4,2,3,4096]{5,3,4,1,2,0:T(2,128)(2,1)} fusion(bf16[32,1,4,2,3,4096]{5,3,4,1,2,0:T(2,128)(2,1)S(1)} %bitcast.68, bf16[32,1,4,2,3,4096]{5,3,4,1,2,0:T(2,128)(2,1)S(1)} %bitcast.69), kind=kLoop, calls=%fused_computation.2 | loop fusion | flops 6291456 | bytes 25165824 | tf_op jit(solution)/shard_map/stack | solution.py:95
  321.9 0.0 all-reduce.2.cloned.1.call-update
  321.9 0.6 copy-done.6
  322.5 0.1 copy.45
  322.6 130.8 %all-reduce.2.cloned.1.call-done = bf16[32,2,4,2,3,4096]{5,3,4,1,2,0:T(2,128)(2,1)} async-done(((bf16[32,2,4,2,3,4096]{5,3,4,1,2,0:T(2,128)(2,1)}), bf16[32,2,4,2,3,4096]{5,3,4,1,2,0:T(2,128)(2,1)}) %all-reduce.2.cloned.1.call-update) | async-done | bytes 12582928 | tf_op jit(solution)/shard_map/psum | solution.py:102
  453.4 2.1 fusion.31
  455.6 4.0 all-to-all-start.3
  459.6 0.0 copy-start.5
  459.6 8.4 %all-to-all-done.3 = bf16[2,4,2,3,4096]{4,2,3,0,1:T(2,128)(2,1)S(1)} async-done(((bf16[2,4,2,3,4096]{4,2,3,0,1:T(2,128)(2,1)}), bf16[2,4,2,3,4096]{4,2,3,0,1:T(2,128)(2,1)S(1)}, u32[]{:S(2)}, u32[]{:S(2)}) %all-to-all-start.3) | async-done | bytes 393248 | tf_op jit(solution)/shard_map/all_to_all | solution.py:104
  467.9 0.3 fusion.58
  468.3 0.3 copy.46
  468.5 0.2 reshape_squeeze.15
  468.8 0.3 copy.44
  469.0 0.2 reshape_squeeze.14
  469.2 0.6 gather_fusion.1
  469.9 0.6 gather_fusion
  470.5 0.1 broadcast_select_fusion.1
  470.6 0.2 reshape.50
  470.8 0.2 reshape.51
  471.0 0.7 multiply_reduce_fusion
  471.7 2.5 collective-permute-start.1
  474.3 0.6 add_convert_fusion.1
  474.9 6.2 %collective-permute-done.1 = bf16[3,4096]{1,0:T(4,128)(2,1)S(1)} collective-permute-done((bf16[3,4096]{1,0:T(4,128)(2,1)S(1)}, bf16[3,4096]{1,0:T(4,128)(2,1)S(1)}, u32[]{:S(2)}, u32[]{:S(2)}) %collective-permute-start.1) | collective-permute-done | bytes 24608 | tf_op jit(solution)/shard_map/ppermute | solution.py:10
  481.2 0.7 fusion.41
  (30 shorter events, 0.1 us)
Async XLA Ops:
  8.0 11.4 %collective-permute-start = (bf16[3,4096]{1,0:T(4,128)(2,1)S(1)}, bf16[3,4096]{1,0:T(4,128)(2,1)S(1)}, u32[]{:S(2)}, u32[]{:S(2)}) collective-permute-start(bf16[3,4096]{1,0:T(4,128)(2,1)S(1)} %slice.55), channel_id=1, source_target_pairs={{0,1},{1,2},{2,3},{3,4},{4,5},{5,6},{6,7},{7,8},{8,9},{9,10},{10,1... | collective-permute-start | bytes 73736 | tf_op jit(solution)/shard_map/ppermute | solution.py:10
  13.6 9.1 %all-to-all-start.1 = ((bf16[4,2,3,4096]{3,1,2,0:T(2,128)(2,1)}), bf16[4,2,3,4096]{3,1,2,0:T(2,128)(2,1)S(1)}, u32[]{:S(2)}, u32[]{:S(2)}) async-start(bf16[4,2,3,4096]{3,1,2,0:T(2,128)(2,1)} %copy.38), calls=%async_computation.1 | async-start | bytes 393216 | tf_op jit(solution)/shard_map/all_to_all | solution.py:82
  17.5 435.9 %all-reduce.2.cloned.1.call-start = ((), (), s32[]{:S(2)}) async-start(), calls=%async_computation.4 | async-start | bytes 25165824 | tf_op jit(solution)/shard_map/psum | solution.py:102
  209.3 9.7 %copy-start.1 = (bf16[128,2,3,4096]{3,0,2,1:T(8,128)(2,1)S(1)}, bf16[128,2,3,4096]{3,0,2,1:T(8,128)(2,1)}, u32[]{:S(2)}) copy-start(bf16[128,2,3,4096]{3,0,2,1:T(8,128)(2,1)} %reshape_squeeze.12) | copy-start | bytes 18874372
  209.4 16.9 %slice-start = ((s8[6291456]{0:T(1024)(128)(4,1)}), s8[4194304]{0:T(1024)(128)(4,1)S(1)}, s32[]{:S(2)}) async-start(s8[6291456]{0:T(1024)(128)(4,1)} %bitcast.66), calls=%async_computation.5 | async-start | bytes 8388608
  219.1 7.2 %slice-start.1 = ((s8[6291456]{0:T(1024)(128)(4,1)}), s8[2097152]{0:T(1024)(128)(4,1)S(1)}, s32[]{:S(2)}) async-start(s8[6291456]{0:T(1024)(128)(4,1)} %bitcast.66), calls=%async_computation.6 | async-start | bytes 4194304
  232.0 28.3 %slice-start.2 = ((s8[7340032]{0:T(1024)(128)(4,1)}), s8[3145728]{0:T(1024)(128)(4,1)S(1)}, s32[]{:S(2)}) async-start(s8[7340032]{0:T(1024)(128)(4,1)} %bitcast.70), calls=%async_computation.7 | async-start | bytes 6291456
  241.9 8.7 %copy-start.2 = (f32[128,2,3,448]{0,3,2,1:T(8,128)S(1)}, f32[128,2,3,448]{0,3,2,1:T(8,128)}, u32[]{:S(2)}) copy-start(f32[128,2,3,448]{0,3,2,1:T(8,128)} %fusion.23) | copy-start | bytes 4128772
  241.9 8.7 %copy-start.4 = (f32[128,2,3,448]{0,3,2,1:T(8,128)S(1)}, f32[128,2,3,448]{0,3,2,1:T(8,128)}, u32[]{:S(2)}) copy-start(f32[128,2,3,448]{0,3,2,1:T(8,128)} %fusion.26) | copy-start | bytes 4128772
  241.9 18.5 %slice-start.3 = ((s8[7340032]{0:T(1024)(128)(4,1)}), s8[4194304]{0:T(1024)(128)(4,1)S(1)}, s32[]{:S(2)}) async-start(s8[7340032]{0:T(1024)(128)(4,1)} %bitcast.70), calls=%async_computation.8 | async-start | bytes 8388608
  250.6 9.8 %copy-start.3 = (f32[128,2,3,448]{0,3,2,1:T(8,128)}, f32[128,2,3,448]{0,3,2,1:T(8,128)S(1)}, u32[]{:S(2)}) copy-start(f32[128,2,3,448]{0,3,2,1:T(8,128)S(1)} %fusion.20) | copy-start | bytes 4128772
  278.1 12.9 %copy-start = (bf16[128,2,3,4096]{3,0,2,1:T(8,128)(2,1)S(1)}, bf16[128,2,3,4096]{3,0,2,1:T(8,128)(2,1)}, u32[]{:S(2)}) copy-start(bf16[128,2,3,4096]{3,0,2,1:T(8,128)(2,1)} %fusion.17) | copy-start | bytes 18874372
  321.9 0.7 copy-start.6
  455.6 12.4 %all-to-all-start.3 = ((bf16[2,4,2,3,4096]{4,2,3,0,1:T(2,128)(2,1)}), bf16[2,4,2,3,4096]{4,2,3,0,1:T(2,128)(2,1)S(1)}, u32[]{:S(2)}, u32[]{:S(2)}) async-start(bf16[2,4,2,3,4096]{4,2,3,0,1:T(2,128)(2,1)} %fusion.31), calls=%async_computation.3 | async-start | bytes 786432 | tf_op jit(solution)/shard_map/all_to_all | solution.py:104
  459.6 12.1 %copy-start.5 = (bf16[8,4096]{1,0:T(8,128)(2,1)S(1)}, bf16[8,4096]{1,0:T(8,128)(2,1)}, u32[]{:S(2)}) copy-start(bf16[8,4096]{1,0:T(8,128)(2,1)} %param.14) | copy-start | bytes 196612
  471.7 9.5 %collective-permute-start.1 = (bf16[3,4096]{1,0:T(4,128)(2,1)S(1)}, bf16[3,4096]{1,0:T(4,128)(2,1)S(1)}, u32[]{:S(2)}, u32[]{:S(2)}) collective-permute-start(bf16[3,4096]{1,0:T(4,128)(2,1)S(1)} %slice.127), channel_id=1, source_target_pairs={{1,0},{2,1},{3,2},{4,3},{5,4},{6,5},{7,6},{8,7},{9,8},{10,9},{11,1... | collective-permute-start | bytes 73736 | tf_op jit(solution)/shard_map/ppermute | solution.py:10
Sparse Core Ops, SparseCore 0:
  322.0 131.3 all-reduce.1
